TPU v7x, 512 devices: a whole 4x8x8 slice. The times are simulated.
512 devices in a mesh: blk: 32 (over x, y_hi, core), grp: 16 (over z, y_lo).
Axes of the slice: x: 4, y: 8 (y_hi: 4, y_lo: 2; y = y_hi * 2 + y_lo), z: 8, core: 2. Of those that a mesh axis runs over, the one named last changes fastest.
Arguments:
- amplitudes: bfloat16 [4096, 8, 4, 128], P('blk'), may hold values from -6 to 6
- integrals: bfloat16 [256, 4096, 128], P('grp', 'blk'), may hold values from -0.15625 to 0.15625
- virt_energy: float32 [4096], replicated, may hold values from 0.5 to 4
- pair_energy: float32 [8], replicated, may hold values from -3 to -0.5
- offsets: int32 [32, 4], replicated, may hold values from 0 to 31, as said below
Outputs:
- ladder: float32 [4096, 8, 4, 128], P(('blk', 'grp'))
- new_amplitudes: float32 [4096, 8, 4, 128], P(('blk', 'grp'))
Inputs may be any that keep to these rules, and one draw needn't show every extreme that they name: The 4 offsets of one row tile are different; the first 3 are at most 2, the last is larger than 2.
All inputs are finite; a program needn't handle non-finite values.
Results may differ from a plain program's by a relative error of at most 0.0029.
Values may be sent and summed in bfloat16 or wider, within the bound.
No kernel may reach another device: no remote copies, remote signals or barrier semaphores. Data moves between devices by JAX's collectives and lax.ppermute only.
A program may use at most 64 MiB of HBM per device.

v0:
```python
import jax
import jax.numpy as jnp
from jax import lax
from jax.sharding import PartitionSpec as P


def in_blocks(x, dim, devices):
    before, after = (x.shape[:dim], x.shape[dim + 1 :])
    return jnp.moveaxis(x.reshape(*before, devices, -1, *after), dim, 0)


def sum_at_owner(x, axis, dim):
    devices = lax.axis_size(axis)
    blocks = lax.all_to_all(in_blocks(x, dim, devices), axis, 0, 0, tiled=True)
    return jnp.sum(blocks, axis=0)


def local(amplitudes, integrals, virt_energy, pair_energy, offsets):
    tiles = lax.axis_size("blk")
    tile_index = lax.axis_index("blk")
    group_index = lax.axis_index("grp")
    slab_width = integrals.shape[2]
    aux_local = integrals.shape[0]
    pair_count = amplitudes.shape[1]
    slot_count = amplitudes.shape[2]
    own_offsets = lax.dynamic_slice_in_dim(offsets, tile_index, 1, 0)[0]
    cols = (tile_index - own_offsets) % tiles
    piece = lax.all_gather(integrals, "blk", axis=1, tiled=True)
    count = piece.shape[1] // slab_width
    tile_ids = jnp.arange(count, dtype=jnp.int32)
    onehot = (cols[:, None] == tile_ids[None, :]).astype(jnp.bfloat16)
    pieces = piece.reshape(aux_local, count, slab_width, slab_width)
    chosen = jnp.einsum("sj,qjbd->qsbd", onehot, pieces, preferred_element_type=jnp.float32)
    col_blocks = chosen.astype(jnp.bfloat16)
    flattened_rows = amplitudes.reshape(slab_width, pair_count * slot_count * slab_width)
    rows_per_device = slab_width // lax.axis_size("grp")

    def add_aux(aux, total):
        half_split = jnp.dot(
            integrals[aux], flattened_rows, preferred_element_type=jnp.float32
        ).astype(jnp.bfloat16)
        half_split = half_split.reshape(
            rows_per_device * lax.axis_size("grp"), pair_count, slot_count, slab_width
        )
        return total + jnp.einsum(
            "apsd,sbd->apsb", half_split, col_blocks[aux], preferred_element_type=jnp.float32
        )

    total_start_offset = jnp.zeros(
        (rows_per_device * lax.axis_size("grp"), pair_count, slot_count, slab_width), jnp.float32
    )
    ladder = sum_at_owner(lax.fori_loop(0, aux_local, add_aux, total_start_offset), "grp", 0)
    first_row = group_index * rows_per_device
    old_rows = lax.dynamic_slice_in_dim(amplitudes, first_row, rows_per_device, 0).astype(
        jnp.float32
    )
    row_energy = lax.dynamic_slice_in_dim(
        virt_energy, tile_index * slab_width + first_row, rows_per_device, 0
    )
    table = virt_energy.reshape(tiles, slab_width)
    selector = (cols[:, None] == jnp.arange(tiles, dtype=jnp.int32)[None, :]).astype(jnp.float32)
    col_energy = jnp.dot(selector, table, precision=lax.Precision.HIGHEST)
    denom = (
        row_energy[:, None, None, None]
        + col_energy[None, None, :, :]
        - pair_energy[None, :, None, None]
    )
    new_amplitudes = old_rows - ladder / denom
    return (ladder, new_amplitudes)


def solution(mesh):
    placed = (P("blk", None, None, None), P("grp", "blk", None), P(), P(), P())
    return jax.shard_map(
        local,
        mesh=mesh,
        in_specs=placed,
        out_specs=(P(("blk", "grp"), None, None, None), P(("blk", "grp"), None, None, None)),
        check_vma=False,
    )
```

profile of v0, /device:TPU:2, one launch (start us, length us, event | category | flops | bytes accessed | tf_op | source)
XLA Modules:
  0.0 332.7 jit_solution(4653998717116399375)
XLA Ops:
  7.9 1.8 reshape.51
  10.0 128.9 %all-gather.2.cloned.1.call-done = bf16[16,4096,128]{2,1,0:T(8,128)(2,1)} async-done(((bf16[16,128,128]{2,1,0:T(8,128)(2,1)}), bf16[16,4096,128]{2,1,0:T(8,128)(2,1)}) %all-gather.2.cloned.1.call-update) | async-done | bytes 16777232 | tf_op jit(solution)/shard_map/all_gather | solution.py:28
  138.9 16.6 %convert_bitcast_fusion = bf16[16,4,128,128]{3,1,2,0:T(4,128)(2,1)} fusion(bf16[16,32,128,128]{3,2,1,0:T(8,128)(2,1)} %bitcast.32, s32[4]{0:T(128)S(1)} %and_select_fusion), kind=kOutput, calls=%fused_computation.10 | convolution fusion | flops 68157568 | bytes 18874384 | tf_op jit(solution)/shard_map/sj,qjbd->qsbd/dot_general | solution.py:33
  155.5 105.9 %while.14 = (s32[]{:T(128)}, f32[128,8,4,128]{0,3,1,2:T(8,128)}, bf16[16,4,128,128]{3,1,2,0:T(4,128)(2,1)}, bf16[16,128,128]{2,1,0:T(8,128)(2,1)}, bf16[128,4096]{1,0:T(8,128)(2,1)S(1)}, /*index=5*/s32[]{:T(128)}, s32[]{:T(128)}) while((s32[]{:T(128)}, f32[128,8,4,128]{0,3,1,2:T(8,128)}, bf16[16,4,128,128]{3,1,2,0:T(4,128)(2,1)}, ...), condition=%wide.region_1.2_spmd.clone, body=%wide.region_0.1_spmd.clone.sunk | while | flops 270008320 | bytes 9863271 | solution.py:52
  158.4 2.2 bitcast_add_fusion.2
  161.6 1.2 convolution_convert_fusion.2
  163.5 3.8 %bitcast_add_fusion.2 = f32[128,8,4,128]{0,3,1,2:T(8,128)} fusion(f32[128,8,4,128]{0,3,1,2:T(8,128)} %get-tuple-element.181, bf16[128,8,4,128]{3,2,1,0:T(4,128)(2,1)S(1)} %reshape.59, pred[]{:T(512)S(6)} %compare.7, bf16[1,4,128,128]{3,1,2,0:T(4,128)(2,1)S(1)} %constant_dynamic-slice_fusion.3), kind=kOutput, calls=%fused_computation.1.clone.1 | convolution fusion | flops 135266304 | bytes 5373953 | tf_op jit(solution)/shard_map/while/body/eval_jaxpr/apsd,sbd->apsb/dot_general | solution.py:45
  170.2 3.8 %bitcast_add_fusion.2 = f32[128,8,4,128]{0,3,1,2:T(8,128)} fusion(f32[128,8,4,128]{0,3,1,2:T(8,128)} %get-tuple-element.181, bf16[128,8,4,128]{3,2,1,0:T(4,128)(2,1)S(1)} %reshape.59, pred[]{:T(512)S(6)} %compare.7, bf16[1,4,128,128]{3,1,2,0:T(4,128)(2,1)S(1)} %constant_dynamic-slice_fusion.3), kind=kOutput, calls=%fused_computation.1.clone.1 | convolution fusion | flops 135266304 | bytes 5373953 | tf_op jit(solution)/shard_map/while/body/eval_jaxpr/apsd,sbd->apsb/dot_general | solution.py:45
  177.0 3.8 %bitcast_add_fusion.2 = f32[128,8,4,128]{0,3,1,2:T(8,128)} fusion(f32[128,8,4,128]{0,3,1,2:T(8,128)} %get-tuple-element.181, bf16[128,8,4,128]{3,2,1,0:T(4,128)(2,1)S(1)} %reshape.59, pred[]{:T(512)S(6)} %compare.7, bf16[1,4,128,128]{3,1,2,0:T(4,128)(2,1)S(1)} %constant_dynamic-slice_fusion.3), kind=kOutput, calls=%fused_computation.1.clone.1 | convolution fusion | flops 135266304 | bytes 5373953 | tf_op jit(solution)/shard_map/while/body/eval_jaxpr/apsd,sbd->apsb/dot_general | solution.py:45
  183.7 3.8 %bitcast_add_fusion.2 = f32[128,8,4,128]{0,3,1,2:T(8,128)} fusion(f32[128,8,4,128]{0,3,1,2:T(8,128)} %get-tuple-element.181, bf16[128,8,4,128]{3,2,1,0:T(4,128)(2,1)S(1)} %reshape.59, pred[]{:T(512)S(6)} %compare.7, bf16[1,4,128,128]{3,1,2,0:T(4,128)(2,1)S(1)} %constant_dynamic-slice_fusion.3), kind=kOutput, calls=%fused_computation.1.clone.1 | convolution fusion | flops 135266304 | bytes 5373953 | tf_op jit(solution)/shard_map/while/body/eval_jaxpr/apsd,sbd->apsb/dot_general | solution.py:45
  190.4 3.8 %bitcast_add_fusion.2 = f32[128,8,4,128]{0,3,1,2:T(8,128)} fusion(f32[128,8,4,128]{0,3,1,2:T(8,128)} %get-tuple-element.181, bf16[128,8,4,128]{3,2,1,0:T(4,128)(2,1)S(1)} %reshape.59, pred[]{:T(512)S(6)} %compare.7, bf16[1,4,128,128]{3,1,2,0:T(4,128)(2,1)S(1)} %constant_dynamic-slice_fusion.3), kind=kOutput, calls=%fused_computation.1.clone.1 | convolution fusion | flops 135266304 | bytes 5373953 | tf_op jit(solution)/shard_map/while/body/eval_jaxpr/apsd,sbd->apsb/dot_general | solution.py:45
  197.1 3.8 %bitcast_add_fusion.2 = f32[128,8,4,128]{0,3,1,2:T(8,128)} fusion(f32[128,8,4,128]{0,3,1,2:T(8,128)} %get-tuple-element.181, bf16[128,8,4,128]{3,2,1,0:T(4,128)(2,1)S(1)} %reshape.59, pred[]{:T(512)S(6)} %compare.7, bf16[1,4,128,128]{3,1,2,0:T(4,128)(2,1)S(1)} %constant_dynamic-slice_fusion.3), kind=kOutput, calls=%fused_computation.1.clone.1 | convolution fusion | flops 135266304 | bytes 5373953 | tf_op jit(solution)/shard_map/while/body/eval_jaxpr/apsd,sbd->apsb/dot_general | solution.py:45
  203.8 3.8 %bitcast_add_fusion.2 = f32[128,8,4,128]{0,3,1,2:T(8,128)} fusion(f32[128,8,4,128]{0,3,1,2:T(8,128)} %get-tuple-element.181, bf16[128,8,4,128]{3,2,1,0:T(4,128)(2,1)S(1)} %reshape.59, pred[]{:T(512)S(6)} %compare.7, bf16[1,4,128,128]{3,1,2,0:T(4,128)(2,1)S(1)} %constant_dynamic-slice_fusion.3), kind=kOutput, calls=%fused_computation.1.clone.1 | convolution fusion | flops 135266304 | bytes 5373953 | tf_op jit(solution)/shard_map/while/body/eval_jaxpr/apsd,sbd->apsb/dot_general | solution.py:45
  210.5 3.8 %bitcast_add_fusion.2 = f32[128,8,4,128]{0,3,1,2:T(8,128)} fusion(f32[128,8,4,128]{0,3,1,2:T(8,128)} %get-tuple-element.181, bf16[128,8,4,128]{3,2,1,0:T(4,128)(2,1)S(1)} %reshape.59, pred[]{:T(512)S(6)} %compare.7, bf16[1,4,128,128]{3,1,2,0:T(4,128)(2,1)S(1)} %constant_dynamic-slice_fusion.3), kind=kOutput, calls=%fused_computation.1.clone.1 | convolution fusion | flops 135266304 | bytes 5373953 | tf_op jit(solution)/shard_map/while/body/eval_jaxpr/apsd,sbd->apsb/dot_general | solution.py:45
  217.3 3.8 %bitcast_add_fusion.2 = f32[128,8,4,128]{0,3,1,2:T(8,128)} fusion(f32[128,8,4,128]{0,3,1,2:T(8,128)} %get-tuple-element.181, bf16[128,8,4,128]{3,2,1,0:T(4,128)(2,1)S(1)} %reshape.59, pred[]{:T(512)S(6)} %compare.7, bf16[1,4,128,128]{3,1,2,0:T(4,128)(2,1)S(1)} %constant_dynamic-slice_fusion.3), kind=kOutput, calls=%fused_computation.1.clone.1 | convolution fusion | flops 135266304 | bytes 5373953 | tf_op jit(solution)/shard_map/while/body/eval_jaxpr/apsd,sbd->apsb/dot_general | solution.py:45
  224.0 3.8 %bitcast_add_fusion.2 = f32[128,8,4,128]{0,3,1,2:T(8,128)} fusion(f32[128,8,4,128]{0,3,1,2:T(8,128)} %get-tuple-element.181, bf16[128,8,4,128]{3,2,1,0:T(4,128)(2,1)S(1)} %reshape.59, pred[]{:T(512)S(6)} %compare.7, bf16[1,4,128,128]{3,1,2,0:T(4,128)(2,1)S(1)} %constant_dynamic-slice_fusion.3), kind=kOutput, calls=%fused_computation.1.clone.1 | convolution fusion | flops 135266304 | bytes 5373953 | tf_op jit(solution)/shard_map/while/body/eval_jaxpr/apsd,sbd->apsb/dot_general | solution.py:45
  230.7 3.8 %bitcast_add_fusion.2 = f32[128,8,4,128]{0,3,1,2:T(8,128)} fusion(f32[128,8,4,128]{0,3,1,2:T(8,128)} %get-tuple-element.181, bf16[128,8,4,128]{3,2,1,0:T(4,128)(2,1)S(1)} %reshape.59, pred[]{:T(512)S(6)} %compare.7, bf16[1,4,128,128]{3,1,2,0:T(4,128)(2,1)S(1)} %constant_dynamic-slice_fusion.3), kind=kOutput, calls=%fused_computation.1.clone.1 | convolution fusion | flops 135266304 | bytes 5373953 | tf_op jit(solution)/shard_map/while/body/eval_jaxpr/apsd,sbd->apsb/dot_general | solution.py:45
  237.4 3.8 %bitcast_add_fusion.2 = f32[128,8,4,128]{0,3,1,2:T(8,128)} fusion(f32[128,8,4,128]{0,3,1,2:T(8,128)} %get-tuple-element.181, bf16[128,8,4,128]{3,2,1,0:T(4,128)(2,1)S(1)} %reshape.59, pred[]{:T(512)S(6)} %compare.7, bf16[1,4,128,128]{3,1,2,0:T(4,128)(2,1)S(1)} %constant_dynamic-slice_fusion.3), kind=kOutput, calls=%fused_computation.1.clone.1 | convolution fusion | flops 135266304 | bytes 5373953 | tf_op jit(solution)/shard_map/while/body/eval_jaxpr/apsd,sbd->apsb/dot_general | solution.py:45
  244.1 3.8 %bitcast_add_fusion.2 = f32[128,8,4,128]{0,3,1,2:T(8,128)} fusion(f32[128,8,4,128]{0,3,1,2:T(8,128)} %get-tuple-element.181, bf16[128,8,4,128]{3,2,1,0:T(4,128)(2,1)S(1)} %reshape.59, pred[]{:T(512)S(6)} %compare.7, bf16[1,4,128,128]{3,1,2,0:T(4,128)(2,1)S(1)} %constant_dynamic-slice_fusion.3), kind=kOutput, calls=%fused_computation.1.clone.1 | convolution fusion | flops 135266304 | bytes 5373953 | tf_op jit(solution)/shard_map/while/body/eval_jaxpr/apsd,sbd->apsb/dot_general | solution.py:45
  250.8 3.8 %bitcast_add_fusion.2 = f32[128,8,4,128]{0,3,1,2:T(8,128)} fusion(f32[128,8,4,128]{0,3,1,2:T(8,128)} %get-tuple-element.181, bf16[128,8,4,128]{3,2,1,0:T(4,128)(2,1)S(1)} %reshape.59, pred[]{:T(512)S(6)} %compare.7, bf16[1,4,128,128]{3,1,2,0:T(4,128)(2,1)S(1)} %constant_dynamic-slice_fusion.3), kind=kOutput, calls=%fused_computation.1.clone.1 | convolution fusion | flops 135266304 | bytes 5373953 | tf_op jit(solution)/shard_map/while/body/eval_jaxpr/apsd,sbd->apsb/dot_general | solution.py:45
  257.5 3.8 %bitcast_add_fusion.2 = f32[128,8,4,128]{0,3,1,2:T(8,128)} fusion(f32[128,8,4,128]{0,3,1,2:T(8,128)} %get-tuple-element.181, bf16[128,8,4,128]{3,2,1,0:T(4,128)(2,1)S(1)} %reshape.59, pred[]{:T(512)S(6)} %compare.7, bf16[1,4,128,128]{3,1,2,0:T(4,128)(2,1)S(1)} %constant_dynamic-slice_fusion.3), kind=kOutput, calls=%fused_computation.1.clone.1 | convolution fusion | flops 135266304 | bytes 5373953 | tf_op jit(solution)/shard_map/while/body/eval_jaxpr/apsd,sbd->apsb/dot_general | solution.py:45
  261.3 3.1 copy.16
  264.5 8.6 %all-to-all-start = ((f32[16,8,8,4,128]{4,2,3,1,0:T(8,128)}), f32[16,8,8,4,128]{4,2,3,1,0:T(8,128)S(1)}, u32[]{:S(2)}, u32[]{:S(2)}) async-start(f32[16,8,8,4,128]{4,2,3,1,0:T(8,128)} %bitcast.33), calls=%async_computation | async-start | bytes 4194304 | tf_op jit(solution)/shard_map/all_to_all | solution.py:14
  274.3 49.9 %all-to-all-done = f32[16,8,8,4,128]{4,2,3,1,0:T(8,128)S(1)} async-done(((f32[16,8,8,4,128]{4,2,3,1,0:T(8,128)}), f32[16,8,8,4,128]{4,2,3,1,0:T(8,128)S(1)}, u32[]{:S(2)}, u32[]{:S(2)}) %all-to-all-start) | async-done | bytes 2097184 | tf_op jit(solution)/shard_map/all_to_all | solution.py:14
  (66 shorter events, 49.0 us)
Async XLA Ops:
  7.2 2.6 copy-start
  7.2 131.7 %all-gather.2.cloned.1.call-start = ((), (), s32[]{:S(2)}) async-start(), calls=%async_computation.1 | async-start | bytes 17301504 | tf_op jit(solution)/shard_map/all_gather | solution.py:28
  264.5 8.6 %copy-start.2 = (f32[4096]{0:T(1024)S(1)}, f32[4096]{0:T(1024)}, u32[]{:S(2)}) copy-start(f32[4096]{0:T(1024)} %param.9) | copy-start | bytes 49156
  264.5 59.7 %all-to-all-start = ((f32[16,8,8,4,128]{4,2,3,1,0:T(8,128)}), f32[16,8,8,4,128]{4,2,3,1,0:T(8,128)S(1)}, u32[]{:S(2)}, u32[]{:S(2)}) async-start(f32[16,8,8,4,128]{4,2,3,1,0:T(8,128)} %bitcast.33), calls=%async_computation | async-start | bytes 4194304 | tf_op jit(solution)/shard_map/all_to_all | solution.py:14
  273.0 52.0 %copy-start.1 = (f32[8]{0:T(128)S(1)}, f32[8]{0:T(128)}, u32[]{:S(2)}) copy-start(f32[8]{0:T(128)} %param.10) | copy-start | bytes 100
Sparse Core Ops, SparseCore 0:
  11.2 127.5 all-gather.1
where the time goes:
time: 335 us; the launch traced here: 333 us
  waiting for transfers between devices  179 us (53%)
  matrix products  94.9 us (28%)
  local copies, waits for them, and re-layouts  34.7 us (10%)
  between operations  14.1 us (4%)
  starting transfers between devices  8.6 us (3%)
    all_gather x1, waiting for transfers between devices, local(): piece = lax.all_gather(integrals, 'blk', axis=1, tiled=True)  129 us
    dot_general x16, matrix products, add_aux(): jnp.einsum('apsd,sbd->apsb', half_split, col_blocks[aux], preferred_eleme...  59.2 us
    all_to_all x1, waiting for transfers between devices, sum_at_owner(): blocks = lax.all_to_all(in_blocks(x, dim, devices), axis, 0, 0, tiled=True)  49.9 us
    dot_general x16, matrix products, add_aux(): jnp.dot(integrals[aux], flattened_rows, preferred_element_type=jnp.float32)  18.9 us
    dot_general x1, matrix products, local(): jnp.einsum('sj,qjbd->qsbd', onehot, pieces, preferred_element_type=jnp.fl...  16.6 us
    dynamic_slice x16, local copies, waits for them, and re-layouts, add_aux(): col_blocks[aux]  15.2 us
    reshape x16, local copies, waits for them, and re-layouts, add_aux(): half_split.reshape(rows_per_device * lax.axis_size('grp'), pair_count, sl...  12.2 us
    all_to_all x1, starting transfers between devices, sum_at_owner(): blocks = lax.all_to_all(in_blocks(x, dim, devices), axis, 0, 0, tiled=True)  8.57 us
  transfers between devices with their start and end apart: 2, of which 2 were waited for; matrix products, arithmetic and copies ran while one was open for 1% of the time, Pallas kernels for 0%

commit v1 on v0

--- a/solution.py
+++ b/solution.py
@@ -25,7 +25,9 @@
     slot_count = amplitudes.shape[2]
     own_offsets = lax.dynamic_slice_in_dim(offsets, tile_index, 1, 0)[0]
     cols = (tile_index - own_offsets) % tiles
-    piece = lax.all_gather(integrals, "blk", axis=1, tiled=True)
+    piece = jnp.concatenate(
+        lax.all_to_all(jnp.stack([integrals] * lax.axis_size("blk")), "blk", 0, 0), axis=1
+    )
     count = piece.shape[1] // slab_width
     tile_ids = jnp.arange(count, dtype=jnp.int32)
     onehot = (cols[:, None] == tile_ids[None, :]).astype(jnp.bfloat16)

time: 335 us -> 577 us (1.72)
  the two profiles are of different devices: /device:TPU:2 before, /device:TPU:7 now
where the time goes in v1:
time: 577 us; the launch traced here: 575 us
  waiting for transfers between devices  414 us (72%)
  matrix products  95.1 us (16%)
  local copies, waits for them, and re-layouts  40.9 us (7%)
  starting transfers between devices  23.5 us (4%)
    all_to_all x1, waiting for transfers between devices, local(): lax.all_to_all(jnp.stack([integrals] * lax.axis_size('blk')), 'blk', 0, 0)  363 us
    dot_general x16, matrix products, add_aux(): jnp.einsum('apsd,sbd->apsb', half_split, col_blocks[aux], preferred_eleme...  59.4 us
    all_to_all x1, waiting for transfers between devices, sum_at_owner(): blocks = lax.all_to_all(in_blocks(x, dim, devices), axis, 0, 0, tiled=True)  50.5 us
    dot_general x16, matrix products, add_aux(): jnp.dot(integrals[aux], flattened_rows, preferred_element_type=jnp.float32)  18.8 us
    dot_general x1, matrix products, local(): jnp.einsum('sj,qjbd->qsbd', onehot, pieces, preferred_element_type=jnp.fl...  16.6 us
    dynamic_slice x16, local copies, waits for them, and re-layouts, add_aux(): col_blocks[aux]  15.3 us
    all_to_all x1, starting transfers between devices, sum_at_owner(): blocks = lax.all_to_all(in_blocks(x, dim, devices), axis, 0, 0, tiled=True)  12.3 us
    reshape x16, local copies, waits for them, and re-layouts, add_aux(): half_split.reshape(rows_per_device * lax.axis_size('grp'), pair_count, sl...  12.2 us
  transfers between devices with their start and end apart: 2, of which 2 were waited for; matrix products, arithmetic and copies ran while one was open for 0% of the time, Pallas kernels for 0%

profile of v1, /device:TPU:7, one launch (start us, length us, event | category | flops | bytes accessed | tf_op | source)
XLA Modules:
  0.0 574.6 jit_solution(11668012332613712778)
XLA Ops:
  0.6 7.0 %stack.2 = bf16[32,16,128,128]{3,2,1,0:T(8,128)(2,1)} broadcast(bf16[16,128,128]{2,1,0:T(8,128)(2,1)} %param.8), dimensions={1,2,3} | broadcast | bytes 17301504 | tf_op jit(solution)/shard_map/stack | solution.py:29
  7.7 11.1 %all-to-all-start = ((bf16[32,16,128,128]{3,2,1,0:T(8,128)(2,1)}), bf16[32,16,128,128]{3,2,1,0:T(8,128)(2,1)}, u32[]{:S(2)}, u32[]{:S(2)}) async-start(bf16[32,16,128,128]{3,2,1,0:T(8,128)(2,1)} %stack.2), calls=%async_computation | async-start | bytes 33554432 | tf_op jit(solution)/shard_map/all_to_all | solution.py:29
  19.9 363.1 %all-to-all-done = bf16[32,16,128,128]{3,2,1,0:T(8,128)(2,1)} async-done(((bf16[32,16,128,128]{3,2,1,0:T(8,128)(2,1)}), bf16[32,16,128,128]{3,2,1,0:T(8,128)(2,1)}, u32[]{:S(2)}, u32[]{:S(2)}) %all-to-all-start) | async-done | bytes 16777248 | tf_op jit(solution)/shard_map/all_to_all | solution.py:29
  383.0 16.6 %convert_bitcast_fusion = bf16[16,4,128,128]{3,1,2,0:T(4,128)(2,1)} fusion(bf16[32,16,128,128]{3,2,1,0:T(8,128)(2,1)} %all-to-all-done, s32[4]{0:T(128)S(1)} %and_select_fusion), kind=kOutput, calls=%fused_computation.11 | convolution fusion | flops 68157568 | bytes 18874384 | tf_op jit(solution)/shard_map/sj,qjbd->qsbd/dot_general | solution.py:35
  399.6 106.2 %while.14 = (s32[]{:T(128)}, f32[128,8,4,128]{0,3,1,2:T(8,128)}, bf16[16,4,128,128]{3,1,2,0:T(4,128)(2,1)}, bf16[16,128,128]{2,1,0:T(8,128)(2,1)}, bf16[128,4096]{1,0:T(8,128)(2,1)S(1)}, /*index=5*/s32[]{:T(128)}, s32[]{:T(128)}) while((s32[]{:T(128)}, f32[128,8,4,128]{0,3,1,2:T(8,128)}, bf16[16,4,128,128]{3,1,2,0:T(4,128)(2,1)}, ...), condition=%wide.region_1.2_spmd.clone, body=%wide.region_0.1_spmd.clone.sunk | while | flops 270008320 | bytes 9863771 | solution.py:54
  402.5 2.2 bitcast_add_fusion.2
  407.7 3.8 bitcast_add_fusion.2
  414.4 3.8 bitcast_add_fusion.2
  421.2 3.8 bitcast_add_fusion.2
  427.9 3.8 bitcast_add_fusion.2
  434.6 3.8 bitcast_add_fusion.2
  441.4 3.8 bitcast_add_fusion.2
  448.1 3.8 bitcast_add_fusion.2
  454.9 3.8 bitcast_add_fusion.2
  461.6 3.8 bitcast_add_fusion.2
  468.3 3.8 bitcast_add_fusion.2
  475.1 3.8 bitcast_add_fusion.2
  481.8 3.8 bitcast_add_fusion.2
  488.5 3.8 bitcast_add_fusion.2
  495.3 3.8 bitcast_add_fusion.2
  502.0 3.8 bitcast_add_fusion.2
  505.8 3.1 copy.15
  508.9 12.3 %all-to-all-start.1 = ((f32[16,8,8,4,128]{4,2,3,1,0:T(8,128)}), f32[16,8,8,4,128]{4,2,3,1,0:T(8,128)S(1)}, u32[]{:S(2)}, u32[]{:S(2)}) async-start(f32[16,8,8,4,128]{4,2,3,1,0:T(8,128)} %bitcast.36), calls=%async_computation.1 | async-start | bytes 4194304 | tf_op jit(solution)/shard_map/all_to_all | solution.py:14
  522.5 50.5 %all-to-all-done.1 = f32[16,8,8,4,128]{4,2,3,1,0:T(8,128)S(1)} async-done(((f32[16,8,8,4,128]{4,2,3,1,0:T(8,128)}), f32[16,8,8,4,128]{4,2,3,1,0:T(8,128)S(1)}, u32[]{:S(2)}, u32[]{:S(2)}) %all-to-all-start.1) | async-done | bytes 2097184 | tf_op jit(solution)/shard_map/all_to_all | solution.py:14
  (68 shorter events, 50.3 us)
Async XLA Ops:
  7.7 11.2 %copy-start = (bf16[128,8,4,128]{3,2,1,0:T(4,128)(2,1)S(1)}, bf16[128,8,4,128]{3,2,1,0:T(4,128)(2,1)}, u32[]{:S(2)}) copy-start(bf16[128,8,4,128]{3,2,1,0:T(4,128)(2,1)} %param.7) | copy-start | bytes 3145732
  7.7 375.3 %all-to-all-start = ((bf16[32,16,128,128]{3,2,1,0:T(8,128)(2,1)}), bf16[32,16,128,128]{3,2,1,0:T(8,128)(2,1)}, u32[]{:S(2)}, u32[]{:S(2)}) async-start(bf16[32,16,128,128]{3,2,1,0:T(8,128)(2,1)} %stack.2), calls=%async_computation | async-start | bytes 33554432 | tf_op jit(solution)/shard_map/all_to_all | solution.py:29
  18.8 0.9 copy-start.1
  508.9 12.3 %copy-start.3 = (f32[4096]{0:T(1024)S(1)}, f32[4096]{0:T(1024)}, u32[]{:S(2)}) copy-start(f32[4096]{0:T(1024)} %param.9) | copy-start | bytes 49156
  508.9 64.0 %all-to-all-start.1 = ((f32[16,8,8,4,128]{4,2,3,1,0:T(8,128)}), f32[16,8,8,4,128]{4,2,3,1,0:T(8,128)S(1)}, u32[]{:S(2)}, u32[]{:S(2)}) async-start(f32[16,8,8,4,128]{4,2,3,1,0:T(8,128)} %bitcast.36), calls=%async_computation.1 | async-start | bytes 4194304 | tf_op jit(solution)/shard_map/all_to_all | solution.py:14
  521.3 52.6 %copy-start.2 = (f32[8]{0:T(128)S(1)}, f32[8]{0:T(128)}, u32[]{:S(2)}) copy-start(f32[8]{0:T(128)} %param.10) | copy-start | bytes 100
